TPU v7x, 32 devices: a whole 2x2x4 slice. The times are simulated.
32 devices in a mesh: grp: 4 (over z), mem: 8 (over y, x, core).
Axes of the slice: x: 2, y: 2, z: 4, core: 2. Of those that a mesh axis runs over, the one named last changes fastest.
Arguments:
- bin_sketch: bfloat16 [256, 1024], P(('grp', 'mem')), may hold values from -6 to 6
- rep_sketch: bfloat16 [8192, 1024], P(('grp', 'mem')), may hold values from -6 to 6
- bin_profile: bfloat16 [256, 32768], P('grp', 'mem'), may hold values from -6 to 6
- member_profile: bfloat16 [12, 256, 32768], P('grp', None, 'mem'), may hold values from -6 to 6
- bin_routes: int32 [256, 2], P('grp'), may hold values from 0 to 11, all different within a row; in each aligned block of 64 rows (0 to 63, 64 to 127, ...) at most 16 rows name the same one
- owner_slot: int32 [12], replicated, may hold values from 0 to 11, each once
- cluster_sizes: int32 [12], replicated, may hold values from 128 to 256, as said below
Outputs:
- coarse_scores: bfloat16 [256, 8192], P(None, ('grp', 'mem'))
- fine_scores: float32 [256, 2, 256], P('grp', None, 'mem')
Inputs may be any that keep to these rules, and one draw needn't show every extreme that they name: `bin_routes`: within the bins of one index of grp (64 consecutive bins), no cluster is named by more than 16 routes, a bound that some block reaches; the two clusters of a bin differ. `owner_slot`: A permutation. `cluster_sizes`: each a multiple of 128.
All inputs are finite; a program needn't handle non-finite values.
Results may differ from a plain program's by a relative error of at most 0.001.
Values may be sent and summed in bfloat16 or wider, within the bound.
No kernel may reach another device: no remote copies, remote signals or barrier semaphores. Data moves between devices by JAX's collectives and lax.ppermute only.
A program may use at most 128 MiB of HBM per device.

v0:
```python
import jax
import jax.numpy as jnp
from jax import lax
from jax.sharding import PartitionSpec as P

FW = 32768
MOST = 16


def local(
    bin_sketch, rep_sketch, bin_profile, member_profile, bin_routes, owner_slot, cluster_sizes
):
    coarse_scale = bin_sketch.shape[1] ** (-0.5)
    group_rows = lax.all_gather(bin_sketch, "mem", axis=0, tiled=True)
    product = lax.dot_general(
        lax.all_gather(group_rows, "grp", axis=0, tiled=True),
        rep_sketch,
        (((1,), (1,)), ((), ())),
        preferred_element_type=jnp.float32,
    )
    coarse_scores = (product * coarse_scale).astype(jnp.bfloat16)
    rows_here, width_here = bin_profile.shape
    slot_count, members, _ = member_profile.shape
    groups = lax.axis_size("grp")
    cluster_total = owner_slot.shape[0]
    capacity = groups * slot_count * MOST
    route_flat = bin_routes.reshape(-1)
    cluster_ids = jnp.arange(cluster_total, dtype=jnp.int32)
    route_hit = (route_flat[:, None] == cluster_ids[None, :]).astype(jnp.int32)
    storage = jnp.sum(route_hit * owner_slot[None, :], axis=1)
    route_size = jnp.sum(route_hit * cluster_sizes[None, :], axis=1)
    route_rank = jnp.sum((jnp.cumsum(route_hit, axis=0) - route_hit) * route_hit, axis=1)
    slot_index = storage * MOST + route_rank
    source = bin_profile[jnp.arange(route_flat.shape[0], dtype=jnp.int32) // 2]
    outgoing = jnp.zeros((capacity, width_here), jnp.bfloat16).at[slot_index].set(source)
    outgoing = outgoing.reshape(groups, slot_count * MOST, width_here)
    incoming = lax.all_to_all(outgoing, "grp", split_axis=0, concat_axis=0, tiled=True)
    incoming = incoming.reshape(groups, slot_count, MOST, width_here)
    partial_value = jnp.einsum(
        "gsmc,sjc->gsmj", incoming, member_profile, preferred_element_type=jnp.float32
    )
    summed = lax.psum_scatter(partial_value, "mem", scatter_dimension=3, tiled=True)
    returned = lax.all_to_all(summed, "grp", split_axis=0, concat_axis=0, tiled=True)
    member_local = returned.shape[3]
    route_scores = returned.reshape(capacity, member_local)[slot_index] * FW ** (-0.5)
    column = lax.axis_index("mem") * member_local + jnp.arange(member_local, dtype=jnp.int32)
    member_live = column[None, :] < route_size[:, None]
    fine_scores = jnp.where(member_live, route_scores, 0.0).reshape(rows_here, 2, member_local)
    return (coarse_scores, fine_scores)


def solution(mesh):
    return jax.shard_map(
        local,
        mesh=mesh,
        in_specs=(
            P(("grp", "mem"), None),
            P(("grp", "mem"), None),
            P("grp", "mem"),
            P("grp", None, "mem"),
            P("grp", None),
            P(),
            P(),
        ),
        out_specs=(P(None, ("grp", "mem")), P("grp", None, "mem")),
        check_vma=False,
    )
```

profile of v0, /device:TPU:0, one launch (start us, length us, event | category | flops | bytes accessed | tf_op | source)
XLA Modules:
  0.0 133.0 jit_solution(8496143700417119367)
XLA Ops:
  7.2 0.0 copy-start
  7.2 0.8 copy.17
  8.0 0.1 eq.15
  8.2 0.1 fusion.12
  8.3 0.2 reduce_window_sum.11
  8.4 0.9 select_reduce_fusion.2
  9.3 0.0 copy-done
  9.3 6.4 %scatter_custom_fusion = bf16[192,4096]{1,0:T(8,128)(2,1)} fusion(s32[128]{0:T(128)S(1)} %fusion.14, bf16[64,4096]{1,0:T(8,128)(2,1)S(1)} %copy-done, s32[1024]{0:T(1024)S(1)} %pad_clamp_fusion.1, bf16[]{:T(256)} %constant.36.clone.1), kind=kCustom, calls=%fused_computation.9 | custom fusion | bytes 1572866 | tf_op jit(solution)/shard_map/scatter | solution.py:35
  15.7 6.5 %all-to-all-start = ((bf16[4,48,4096]{2,1,0:T(8,128)(2,1)}), bf16[4,48,4096]{2,1,0:T(8,128)(2,1)S(1)}, u32[]{:S(2)}, u32[]{:S(2)}) async-start(bf16[4,48,4096]{2,1,0:T(8,128)(2,1)} %bitcast.3), calls=%async_computation | async-start | bytes 3145728 | tf_op jit(solution)/shard_map/all_to_all | solution.py:37
  22.2 0.0 reduce-scatter.4.cloned.1.call-start
  22.2 9.2 %all_gather.6 = bf16[64,1024]{1,0:T(8,128)(2,1)S(1)} all-gather(bf16[8,1024]{1,0:T(8,128)(2,1)S(1)} %copy-done.2), channel_id=1, replica_groups=mesh['grp'=4,'mem'=8] {'mem'}, dimensions={0}, use_global_device_ids=true | all-gather | bytes 147456 | tf_op jit(solution)/shard_map/all_gather | solution.py:14
  31.4 38.1 %all_gather.7 = bf16[256,1024]{1,0:T(8,128)(2,1)S(1)} all-gather(bf16[64,1024]{1,0:T(8,128)(2,1)S(1)} %all_gather.6), channel_id=1, replica_groups=mesh['grp'=4,'mem'=8] {'grp'}, dimensions={0}, use_global_device_ids=true | all-gather | bytes 655360 | tf_op jit(solution)/shard_map/all_gather | solution.py:16
  69.5 0.0 all-to-all-done
  69.5 4.8 %fusion.4 = f32[4,3,16,256]{3,2,0,1:T(8,128)S(1)} fusion(bf16[3,256,4096]{2,1,0:T(8,128)(2,1)} %param.10, bf16[4,3,16,4096]{3,2,1,0:T(8,128)(2,1)S(1)} %bitcast.25), kind=kOutput, calls=%fused_computation.8 | convolution fusion | flops 402653184 | bytes 8060928 | tf_op jit(solution)/shard_map/gsmc,sjc->gsmj/dot_general | solution.py:39
  74.4 0.7 copy.23
  75.1 1.5 %reshape.132 = f32[256,192]{1,0:T(8,128)} reshape(f32[256,3,4,16]{3,2,1,0:T(4,128)S(1)} %bitcast.24) | data formatting | bytes 393216
  76.6 0.0 reduce-scatter.4.cloned.1.call-update
  76.6 1.0 fusion.3
  77.6 33.7 %reduce-scatter.4.cloned.1.call-done = f32[32,192]{1,0:T(8,128)} async-done(((f32[256,192]{1,0:T(8,128)}), f32[32,192]{1,0:T(8,128)}) %reduce-scatter.4.cloned.1.call-update) | async-done | bytes 24592
  111.4 0.9 reshape.133
  112.3 0.1 copy.20
  112.4 0.7 reshape.140
  113.1 4.6 %all-to-all-start.1 = ((f32[4,1,1536]{2,1,0:T(1,128)}), f32[4,1,1536]{2,1,0:T(1,128)S(1)}, u32[]{:S(2)}, u32[]{:S(2)}) async-start(f32[4,1,1536]{2,1,0:T(1,128)} %reshape.140), calls=%async_computation.1 | async-start | bytes 49152 | tf_op jit(solution)/shard_map/all_to_all | solution.py:43
  117.7 0.1 lt.38
  117.9 0.1 copy.18
  117.9 5.4 %all-to-all-done.1 = f32[4,1,1536]{2,1,0:T(1,128)S(1)} async-done(((f32[4,1,1536]{2,1,0:T(1,128)}), f32[4,1,1536]{2,1,0:T(1,128)S(1)}, u32[]{:S(2)}, u32[]{:S(2)}) %all-to-all-start.1) | async-done | bytes 24608 | tf_op jit(solution)/shard_map/all_to_all | solution.py:43
  123.4 0.5 broadcast.125
  123.9 0.7 reduce
  124.6 0.1 reshape.141
  124.7 0.6 gather_fusion
  125.3 0.1 copy.21
  125.4 0.7 compare_select_fusion
  (10 shorter events, 0.0 us)
Async XLA Ops:
  7.2 2.2 %copy-start = (bf16[64,4096]{1,0:T(8,128)(2,1)S(1)}, bf16[64,4096]{1,0:T(8,128)(2,1)}, u32[]{:S(2)}) copy-start(bf16[64,4096]{1,0:T(8,128)(2,1)} %param.9) | copy-start | bytes 1572868
  15.7 6.5 %copy-start.2 = (bf16[8,1024]{1,0:T(8,128)(2,1)S(1)}, bf16[8,1024]{1,0:T(8,128)(2,1)}, u32[]{:S(2)}) copy-start(bf16[8,1024]{1,0:T(8,128)(2,1)} %param.7) | copy-start | bytes 49156
  15.7 53.8 %all-to-all-start = ((bf16[4,48,4096]{2,1,0:T(8,128)(2,1)}), bf16[4,48,4096]{2,1,0:T(8,128)(2,1)S(1)}, u32[]{:S(2)}, u32[]{:S(2)}) async-start(bf16[4,48,4096]{2,1,0:T(8,128)(2,1)} %bitcast.3), calls=%async_computation | async-start | bytes 3145728 | tf_op jit(solution)/shard_map/all_to_all | solution.py:37
  22.2 89.2 %reduce-scatter.4.cloned.1.call-start = ((), (), s32[]{:S(2)}) async-start(), calls=%async_computation.3 | async-start | bytes 294912
  74.4 2.3 %copy-start.1 = (bf16[256,1024]{1,0:T(8,128)(2,1)S(1)}, bf16[256,1024]{1,0:T(8,128)(2,1)}, u32[]{:S(2)}) copy-start(bf16[256,1024]{1,0:T(8,128)(2,1)} %param.8) | copy-start | bytes 1572868
  113.1 10.2 %all-to-all-start.1 = ((f32[4,1,1536]{2,1,0:T(1,128)}), f32[4,1,1536]{2,1,0:T(1,128)S(1)}, u32[]{:S(2)}, u32[]{:S(2)}) async-start(f32[4,1,1536]{2,1,0:T(1,128)} %reshape.140), calls=%async_computation.1 | async-start | bytes 49152 | tf_op jit(solution)/shard_map/all_to_all | solution.py:43
Sparse Core Ops, SparseCore 0:
  76.7 34.6 reduce-scatter.3
where the time goes:
time: 133 us
  blocking collectives  47.3 us (36%)
  waiting for transfers between devices  39.2 us (29%)
  between operations  14.1 us (11%)
  local copies, waits for them, and re-layouts  12.8 us (10%)
  starting transfers between devices  11.1 us (8%)
  matrix products  5.81 us (4%)
  other arithmetic  2.59 us (2%)
    all_gather x1, blocking collectives, local(): lax.all_gather(group_rows, 'grp', axis=0, tiled=True)  38.1 us
    unnamed x2, waiting for transfers between devices  33.8 us
    all_gather x1, blocking collectives, local(): group_rows = lax.all_gather(bin_sketch, 'mem', axis=0, tiled=True)  9.22 us
    all_to_all x1, starting transfers between devices, local(): lax.all_to_all(outgoing, 'grp', split_axis=0, concat_axis=0, tiled=True)  6.48 us
    scatter x1, local copies, waits for them, and re-layouts, local(): jnp.zeros((capacity, width_here), jnp.bfloat16).at[slot_index].set(source)  6.38 us
    all_to_all x1, waiting for transfers between devices, local(): lax.all_to_all(summed, 'grp', split_axis=0, concat_axis=0, tiled=True)  5.43 us
    dot_general x1, matrix products, local(): jnp.einsum('gsmc,sjc->gsmj', incoming, member_profile, preferred_element_...  4.81 us
    unnamed x12, local copies, waits for them, and re-layouts  4.76 us
  transfers between devices with their start and end apart: 3, of which 2 were waited for; matrix products, arithmetic and copies ran while one was open for 1% of the time, Pallas kernels for 0%

commit v1 on v0

--- a/solution.py
+++ b/solution.py
@@ -40,7 +40,27 @@
         "gsmc,sjc->gsmj", incoming, member_profile, preferred_element_type=jnp.float32
     )
     summed = lax.psum_scatter(partial_value, "mem", scatter_dimension=3, tiled=True)
-    returned = lax.all_to_all(summed, "grp", split_axis=0, concat_axis=0, tiled=True)
+    state_now, v_next = (jax.lax.psum(1, axis_name="grp"), jax.lax.axis_index("grp"))
+    g_now = summed.shape[0] // state_now
+    x_new = list(summed.shape)
+    x_new[0] = g_now
+    everything = x_new[0]
+    x_new[0] = everything * state_now
+    returned = jnp.zeros(x_new, summed.dtype)
+    rr = 0
+    while rr < state_now:
+        big = lax.dynamic_slice_in_dim(summed, (v_next ^ rr) * g_now, g_now, axis=0)
+        if rr:
+            kept_rows = []
+            k0 = 0
+            while k0 < state_now:
+                kept_rows.append((k0, k0 ^ rr))
+                k0 += 1
+            big = jax.lax.ppermute(big, axis_name="grp", perm=kept_rows)
+        returned = lax.dynamic_update_slice_in_dim(
+            returned, big, (v_next ^ rr) * everything, axis=0
+        )
+        rr += 1
     member_local = returned.shape[3]
     route_scores = returned.reshape(capacity, member_local)[slot_index] * FW ** (-0.5)
     column = lax.axis_index("mem") * member_local + jnp.arange(member_local, dtype=jnp.int32)

time: 133 us -> 131 us (0.985)
    all_to_all x1 -> x0, waiting for transfers between devices: 5.43 us -> none  [local(): lax.all_to_all(summed, 'grp', split_axis=0, concat_axis=0, tiled=True)]
    ppermute x0 -> x3, waiting for transfers between devices: none -> 5.08 us  [local(): big = jax.lax.ppermute(big, axis_name='grp', perm=kept_rows)]
    all_to_all x1 -> x0, starting transfers between devices: 4.6 us -> none  [local(): lax.all_to_all(summed, 'grp', split_axis=0, concat_axis=0, tiled=True)]
    ppermute x0 -> x3, starting transfers between devices: none -> 4.42 us  [local(): big = jax.lax.ppermute(big, axis_name='grp', perm=kept_rows)]
    unnamed x12 -> x14, local copies, waits for them, and re-layouts: 4.76 us -> 4.26 us
  transfers between devices with their start and end apart: 3 -> 5, of which waited for: 2 -> 3; matrix products, arithmetic and copies ran while one was open for 1% -> 1% of each run, Pallas kernels for 0% -> 0%
where the time goes in v1:
time: 131 us
  blocking collectives  47.3 us (36%)
  waiting for transfers between devices  38.6 us (29%)
  between operations  14.2 us (11%)
  local copies, waits for them, and re-layouts  11.9 us (9%)
  starting transfers between devices  10.9 us (8%)
  matrix products  5.83 us (4%)
  other arithmetic  1.88 us (1%)
    all_gather x1, blocking collectives, local(): lax.all_gather(group_rows, 'grp', axis=0, tiled=True)  38.1 us
    unnamed x2, waiting for transfers between devices  33.5 us
    all_gather x1, blocking collectives, local(): group_rows = lax.all_gather(bin_sketch, 'mem', axis=0, tiled=True)  9.22 us
    all_to_all x1, starting transfers between devices, local(): lax.all_to_all(outgoing, 'grp', split_axis=0, concat_axis=0, tiled=True)  6.48 us
    scatter x1, local copies, waits for them, and re-layouts, local(): jnp.zeros((capacity, width_here), jnp.bfloat16).at[slot_index].set(source)  6.38 us
    ppermute x3, waiting for transfers between devices, local(): big = jax.lax.ppermute(big, axis_name='grp', perm=kept_rows)  5.08 us
    dot_general x1, matrix products, local(): jnp.einsum('gsmc,sjc->gsmj', incoming, member_profile, preferred_element_...  4.81 us
    ppermute x3, starting transfers between devices, local(): big = jax.lax.ppermute(big, axis_name='grp', perm=kept_rows)  4.42 us
  transfers between devices with their start and end apart: 5, of which 3 were waited for; matrix products, arithmetic and copies ran while one was open for 1% of the time, Pallas kernels for 0%

profile of v1, /device:TPU:0, one launch (start us, length us, event | category | flops | bytes accessed | tf_op | source)
XLA Modules:
  0.0 130.6 jit_solution(6148901632472915457)
XLA Ops:
  7.2 0.0 copy-start
  7.2 0.8 copy.20
  8.0 0.1 eq.15
  8.1 0.1 fusion.12
  8.2 0.2 reduce_window_sum.11
  8.4 0.9 select_reduce_fusion.2
  9.3 6.4 %scatter_custom_fusion = bf16[192,4096]{1,0:T(8,128)(2,1)} fusion(s32[128]{0:T(128)S(1)} %get-tuple-element.10, bf16[64,4096]{1,0:T(8,128)(2,1)S(1)} %copy-done, s32[1024]{0:T(1024)S(1)} %pad_clamp_fusion.1, bf16[]{:T(256)} %constant.44.clone.1), kind=kCustom, calls=%fused_computation.9 | custom fusion | bytes 1572866 | tf_op jit(solution)/shard_map/scatter | solution.py:35
  15.7 6.5 %all-to-all-start = ((bf16[4,48,4096]{2,1,0:T(8,128)(2,1)}), bf16[4,48,4096]{2,1,0:T(8,128)(2,1)S(1)}, u32[]{:S(2)}, u32[]{:S(2)}) async-start(bf16[4,48,4096]{2,1,0:T(8,128)(2,1)} %bitcast.3), calls=%async_computation | async-start | bytes 3145728 | tf_op jit(solution)/shard_map/all_to_all | solution.py:37
  22.2 9.2 %all_gather.6 = bf16[64,1024]{1,0:T(8,128)(2,1)S(1)} all-gather(bf16[8,1024]{1,0:T(8,128)(2,1)S(1)} %copy-done.2), channel_id=1, replica_groups=mesh['grp'=4,'mem'=8] {'mem'}, dimensions={0}, use_global_device_ids=true | all-gather | bytes 147456 | tf_op jit(solution)/shard_map/all_gather | solution.py:14
  31.4 38.1 %all_gather.7 = bf16[256,1024]{1,0:T(8,128)(2,1)S(1)} all-gather(bf16[64,1024]{1,0:T(8,128)(2,1)S(1)} %all_gather.6), channel_id=1, replica_groups=mesh['grp'=4,'mem'=8] {'grp'}, dimensions={0}, use_global_device_ids=true | all-gather | bytes 655360 | tf_op jit(solution)/shard_map/all_gather | solution.py:16
  69.5 4.8 %fusion.4 = f32[4,3,16,256]{3,2,0,1:T(8,128)S(1)} fusion(bf16[3,256,4096]{2,1,0:T(8,128)(2,1)} %param.10, bf16[4,3,16,4096]{3,2,1,0:T(8,128)(2,1)S(1)} %bitcast.33), kind=kOutput, calls=%fused_computation.8 | convolution fusion | flops 402653184 | bytes 8060928 | tf_op jit(solution)/shard_map/gsmc,sjc->gsmj/dot_general | solution.py:39
  74.4 0.7 copy.29
  75.1 1.5 %reshape.132 = f32[256,192]{1,0:T(8,128)} reshape(f32[256,3,4,16]{3,2,1,0:T(4,128)S(1)} %bitcast.32) | data formatting | bytes 393216
  76.6 0.0 reduce-scatter.4.cloned.1.call-update
  76.6 0.1 lt.54
  76.8 0.1 copy.21
  76.8 1.0 fusion.3
  77.8 33.5 %reduce-scatter.4.cloned.1.call-done = f32[32,192]{1,0:T(8,128)} async-done(((f32[256,192]{1,0:T(8,128)}), f32[32,192]{1,0:T(8,128)}) %reduce-scatter.4.cloned.1.call-update) | async-done | bytes 24592
  111.4 0.9 reshape.133
  112.3 0.2 constant_dynamic-slice_fusion
  112.5 0.1 copy.31
  112.5 0.1 copy.32
  112.6 1.5 %collective-permute-start = (f32[1,3,16,32]{3,2,0,1:T(8,128)S(1)}, f32[1,3,16,32]{3,2,0,1:T(8,128)S(1)}, u32[]{:S(2)}, u32[]{:S(2)}) collective-permute-start(f32[1,3,16,32]{3,2,0,1:T(8,128)S(1)} %copy.32), channel_id=1, source_target_pairs={{0,8},{8,0},{16,24},{24,16},{1,9},{9,1},{17,25},{25,17},{2,10},{10... | collective-permute-start | bytes 18440 | tf_op jit(solution)/shard_map/ppermute | solution.py:59
  114.1 0.1 copy.33
  114.2 2.4 %collective-permute-start.1 = (f32[1,3,16,32]{3,2,0,1:T(8,128)S(1)}, f32[1,3,16,32]{3,2,0,1:T(8,128)S(1)}, u32[]{:S(2)}, u32[]{:S(2)}) collective-permute-start(f32[1,3,16,32]{3,2,0,1:T(8,128)S(1)} %copy.33), channel_id=1, source_target_pairs={{0,16},{8,24},{16,0},{24,8},{1,17},{9,25},{17,1},{25,9},{2,18},{10... | collective-permute-start | bytes 18440 | tf_op jit(solution)/shard_map/ppermute | solution.py:59
  116.6 0.1 copy.34
  116.7 0.5 collective-permute-start.2
  117.2 1.9 %collective-permute-done.1 = f32[1,3,16,32]{3,2,0,1:T(8,128)S(1)} collective-permute-done((f32[1,3,16,32]{3,2,0,1:T(8,128)S(1)}, f32[1,3,16,32]{3,2,0,1:T(8,128)S(1)}, u32[]{:S(2)}, u32[]{:S(2)}) %collective-permute-start.1) | collective-permute-done | bytes 6176 | tf_op jit(solution)/shard_map/ppermute | solution.py:59
  119.2 3.1 %collective-permute-done.2 = f32[1,3,16,32]{3,2,0,1:T(8,128)S(1)} collective-permute-done((f32[1,3,16,32]{3,2,0,1:T(8,128)S(1)}, f32[1,3,16,32]{3,2,0,1:T(8,128)S(1)}, u32[]{:S(2)}, u32[]{:S(2)}) %collective-permute-start.2) | collective-permute-done | bytes 6176 | tf_op jit(solution)/shard_map/ppermute | solution.py:59
  122.3 0.6 gather_fusion
  123.0 0.1 copy.27
  123.1 0.7 compare_select_fusion
  (18 shorter events, 0.1 us)
Async XLA Ops:
  7.2 2.2 %copy-start = (bf16[64,4096]{1,0:T(8,128)(2,1)S(1)}, bf16[64,4096]{1,0:T(8,128)(2,1)}, u32[]{:S(2)}) copy-start(bf16[64,4096]{1,0:T(8,128)(2,1)} %param.9) | copy-start | bytes 1572868
  15.7 6.5 %copy-start.2 = (bf16[8,1024]{1,0:T(8,128)(2,1)S(1)}, bf16[8,1024]{1,0:T(8,128)(2,1)}, u32[]{:S(2)}) copy-start(bf16[8,1024]{1,0:T(8,128)(2,1)} %param.7) | copy-start | bytes 49156
  15.7 53.8 %all-to-all-start = ((bf16[4,48,4096]{2,1,0:T(8,128)(2,1)}), bf16[4,48,4096]{2,1,0:T(8,128)(2,1)S(1)}, u32[]{:S(2)}, u32[]{:S(2)}) async-start(bf16[4,48,4096]{2,1,0:T(8,128)(2,1)} %bitcast.3), calls=%async_computation | async-start | bytes 3145728 | tf_op jit(solution)/shard_map/all_to_all | solution.py:37
  22.2 89.2 %reduce-scatter.4.cloned.1.call-start = ((), (), s32[]{:S(2)}) async-start(), calls=%async_computation.2 | async-start | bytes 294912
  74.3 2.5 %copy-start.1 = (bf16[256,1024]{1,0:T(8,128)(2,1)S(1)}, bf16[256,1024]{1,0:T(8,128)(2,1)}, u32[]{:S(2)}) copy-start(bf16[256,1024]{1,0:T(8,128)(2,1)} %param.8) | copy-start | bytes 1572868
  112.6 4.6 %collective-permute-start = (f32[1,3,16,32]{3,2,0,1:T(8,128)S(1)}, f32[1,3,16,32]{3,2,0,1:T(8,128)S(1)}, u32[]{:S(2)}, u32[]{:S(2)}) collective-permute-start(f32[1,3,16,32]{3,2,0,1:T(8,128)S(1)} %copy.32), channel_id=1, source_target_pairs={{0,8},{8,0},{16,24},{24,16},{1,9},{9,1},{17,25},{25,17},{2,10},{10... | collective-permute-start | bytes 18440 | tf_op jit(solution)/shard_map/ppermute | solution.py:59
  114.2 5.0 %collective-permute-start.1 = (f32[1,3,16,32]{3,2,0,1:T(8,128)S(1)}, f32[1,3,16,32]{3,2,0,1:T(8,128)S(1)}, u32[]{:S(2)}, u32[]{:S(2)}) collective-permute-start(f32[1,3,16,32]{3,2,0,1:T(8,128)S(1)} %copy.33), channel_id=1, source_target_pairs={{0,16},{8,24},{16,0},{24,8},{1,17},{9,25},{17,1},{25,9},{2,18},{10... | collective-permute-start | bytes 18440 | tf_op jit(solution)/shard_map/ppermute | solution.py:59
  116.7 5.6 %collective-permute-start.2 = (f32[1,3,16,32]{3,2,0,1:T(8,128)S(1)}, f32[1,3,16,32]{3,2,0,1:T(8,128)S(1)}, u32[]{:S(2)}, u32[]{:S(2)}) collective-permute-start(f32[1,3,16,32]{3,2,0,1:T(8,128)S(1)} %copy.34), channel_id=1, source_target_pairs={{0,24},{8,16},{16,8},{24,0},{1,25},{9,17},{17,9},{25,1},{2,26},{10... | collective-permute-start | bytes 18440 | tf_op jit(solution)/shard_map/ppermute | solution.py:59
Sparse Core Ops, SparseCore 0:
  76.7 34.6 reduce-scatter.3
